TPU v7x, 32 devices: a whole 2x2x4 slice. The times are simulated.
32 devices in a mesh: groups: 2 (over y), chan: 8 (over z, x), win: 2 (over core).
Axes of the slice: x: 2, y: 2, z: 4, core: 2. Of those that a mesh axis runs over, the one named last changes fastest.
Arguments:
- records: bfloat16 [8192, 512], P(('groups', 'chan', 'win')), parts along dimension 0
- record_channel: int32 [8192], P(('groups', 'chan', 'win')), parts along dimension 0, may hold values from 0 to 127, as said below
- record_piece: int32 [8192], P(('groups', 'chan', 'win')), parts along dimension 0, may hold values from 0 to 15
- fir_taps: bfloat16 [32], replicated, may hold values from -1 to 1
- window_starts: int32 [32], P(('groups', 'win')), parts along dimension 0, may hold values from 0 to 1024, as said below
- source_slot: int32 [16], P(('groups', 'chan')), parts along dimension 0, may hold values from 0 to 15
Outputs:
- correlations: float32 [16, 128, 256], P(('groups', 'win'), 'chan'), parts along dimension 0
There are 2 independent parts, one for each index of `groups`. A program takes and returns all parts, laid end to end along the dimension named above; an argument that names none is the same for every part. Nothing has to cross between parts.
Inputs may be any that keep to these rules, and one draw needn't show every extreme that they name: `record_channel`: record r sits on the device r // 256 of chan and win joined, chan slowest. Among the records of one time span each pair of a channel and a piece occurs exactly once. The records of one device hold at most 64 records whose channels lie in any one block of 16 consecutive channels, and in every span some device holds exactly 64 of one block. `window_starts`: window w belongs to span w // 8; the first window of the minute starts at 0 and the last at 1024.
All inputs are finite; a program needn't handle non-finite values.
Results may differ from a plain program's by a relative error of at most 0.0041.
Values may be sent and summed in bfloat16 or wider, within the bound.
No kernel may reach another device: no remote copies, remote signals or barrier semaphores. Data moves between devices by JAX's collectives and lax.ppermute only.
A program may use at most 64 MiB of HBM per device.

v0:
```python
import math
import jax
import jax.numpy as jnp
from jax import lax
from jax.sharding import PartitionSpec as P

CH_DEV = 16
SPAN = 2048
WIN_DEV = 8
WL = 1024
NF = 512
DEC = 4
TAPS = 32
SPILL = 7
SEG = 512
PIECES = 16
BAND = 64
LAGS = 256
EPSILON = 1e-06


def make_filter(fir_taps):
    outputs_per = SEG // DEC
    sample_index = jnp.arange(SEG, dtype=jnp.int32)[:, None]
    column_index = jnp.arange(outputs_per + SPILL, dtype=jnp.int32)[None, :]
    tap_index = jnp.where(
        column_index < outputs_per,
        DEC * column_index + DEC - 1 - sample_index,
        DEC * (column_index - outputs_per) + DEC - 1 + SEG - sample_index,
    )
    match_table = (
        tap_index[:, :, None] == jnp.arange(TAPS, dtype=jnp.int32)[None, None, :]
    ).astype(jnp.float32)
    return jnp.sum(match_table * fir_taps.astype(jnp.float32)[None, None, :], axis=2).astype(
        jnp.bfloat16
    )


def make_fourier():
    sample_index = jnp.arange(WL, dtype=jnp.int32)[:, None]
    freq_index = jnp.arange(NF, dtype=jnp.int32)[None, :]
    phase = 2.0 * math.pi * (sample_index * freq_index % WL).astype(jnp.float32) / WL
    return jnp.concatenate([jnp.cos(phase), -jnp.sin(phase)], axis=1).astype(jnp.bfloat16)


def make_taper():
    sample_index = jnp.arange(WL, dtype=jnp.int32).astype(jnp.float32)
    return 0.5 - 0.5 * jnp.cos(2.0 * math.pi * sample_index / WL)


def make_lags():
    freq_index = jnp.arange(NF, dtype=jnp.int32)[:, None]
    lag_index = jnp.arange(LAGS, dtype=jnp.int32)[None, :] - LAGS // 2
    phase = 2.0 * math.pi * (freq_index * lag_index % WL).astype(jnp.float32) / WL
    scale = 1.0 / math.sqrt(WL * WIN_DEV)
    return (jnp.concatenate([jnp.cos(phase), -jnp.sin(phase)], axis=0) * scale).astype(jnp.bfloat16)


def whiten(spectra):
    freq_index = jnp.arange(NF, dtype=jnp.int32)
    band_table = (jnp.abs(freq_index[:, None] - freq_index[None, :]) <= BAND).astype(jnp.float32)
    band_count = jnp.sum(band_table, axis=0)
    real_part = spectra[..., :NF]
    imag_part = spectra[..., NF:]
    energy = real_part * real_part + imag_part * imag_part
    smooth = jnp.dot(energy, band_table, precision=lax.Precision.HIGHEST) / band_count[None, :]
    amplitude = jnp.sqrt(smooth + EPSILON)
    return (spectra / jnp.concatenate([amplitude, amplitude], axis=-1)).astype(jnp.bfloat16)


def cross_spectrum(source_block, local_block):
    src_real = source_block[..., :NF]
    src_imag = source_block[..., NF:]
    loc_real = local_block[..., :NF]
    loc_imag = local_block[..., NF:]
    real_sum = jnp.einsum(
        "bwf,cwf->bcf", src_real, loc_real, preferred_element_type=jnp.float32
    ) + jnp.einsum("bwf,cwf->bcf", src_imag, loc_imag, preferred_element_type=jnp.float32)
    imag_sum = jnp.einsum(
        "bwf,cwf->bcf", src_imag, loc_real, preferred_element_type=jnp.float32
    ) - jnp.einsum("bwf,cwf->bcf", src_real, loc_imag, preferred_element_type=jnp.float32)
    return jnp.concatenate([real_sum, imag_sum], axis=-1).astype(jnp.bfloat16)


def over_blocks(block_fn, sources, channel_count):
    source_count = sources.shape[0]
    block_size = math.gcd(source_count, 16)
    block_count = source_count // block_size
    grouped = sources.reshape((block_count, block_size) + sources.shape[1:])
    return lax.map(block_fn, grouped).reshape(source_count, channel_count, LAGS)


def body(records, record_channel, record_piece, fir_taps, window_starts, source_slot):
    block_total = lax.axis_size("chan")
    per_device = records.shape[0]
    capacity = 2 * per_device // block_total
    outputs_per = SEG // DEC
    owner_block = record_channel // CH_DEV
    local_slot = record_channel % CH_DEV * PIECES + record_piece
    one_hot = (owner_block[:, None] == jnp.arange(block_total, dtype=jnp.int32)[None, :]).astype(
        jnp.int32
    )
    earlier_count = jnp.sum((jnp.cumsum(one_hot, axis=0) - one_hot) * one_hot, axis=1)
    position = owner_block * capacity + earlier_count
    slot_table = (
        jnp.full((block_total * capacity,), -1, jnp.int32)
        .at[position]
        .set(local_slot)
        .reshape(block_total, capacity)
    )
    filter_matrix = make_filter(fir_taps)
    row_send = (
        jnp.zeros((block_total * capacity, SEG), jnp.bfloat16)
        .at[position]
        .set(records)
        .reshape(block_total, capacity, SEG)
    )
    rows_got, slots_got = (
        lax.all_to_all(row_send, "chan", split_axis=0, concat_axis=0, tiled=True),
        lax.all_to_all(slot_table, "chan", split_axis=0, concat_axis=0, tiled=True),
    )
    flat_slots = slots_got.reshape(-1)
    target = jnp.where(flat_slots >= 0, flat_slots, per_device)
    traces = (
        jnp.zeros((per_device, SEG), jnp.bfloat16)
        .at[target]
        .set(rows_got.reshape(-1, SEG), mode="drop")
    )
    filtered = jnp.dot(traces, filter_matrix, preferred_element_type=jnp.float32)
    main_part = filtered[:, :outputs_per]
    spill_part = filtered[:, outputs_per:]
    main_part = main_part.reshape(CH_DEV, PIECES, outputs_per)
    spill_part = spill_part.reshape(CH_DEV, PIECES, SPILL)
    carried = jnp.pad(spill_part[:, :-1, :], ((0, 0), (1, 0), (0, outputs_per - SPILL)))
    decimated = (main_part + carried).reshape(CH_DEV, SPAN)

    def window_cut(window_start):
        return lax.dynamic_slice_in_dim(decimated, window_start, WL, 1)

    segments = (jax.vmap(window_cut, out_axes=1)(window_starts) * make_taper()).astype(jnp.bfloat16)
    window_count = segments.shape[1]
    spectra = jnp.dot(segments.reshape(-1, WL), make_fourier(), preferred_element_type=jnp.float32)
    whitened = whiten(spectra).reshape(CH_DEV, window_count, WL)
    source = lax.dynamic_slice_in_dim(whitened, source_slot[0], 1, 0)
    gathered = lax.all_gather(source, "chan", axis=0, tiled=True)
    lag_table = make_lags()

    def span_block(source_block):
        cross_spectra = cross_spectrum(source_block, whitened)
        return jnp.dot(
            cross_spectra.reshape(-1, WL), lag_table, preferred_element_type=jnp.float32
        ).reshape(source_block.shape[0], CH_DEV, LAGS)

    return lax.psum_scatter(
        over_blocks(span_block, gathered, CH_DEV), "win", scatter_dimension=0, tiled=True
    )


def solution(mesh):
    in_specs = (
        P(("groups", "chan", "win"), None),
        P(("groups", "chan", "win")),
        P(("groups", "chan", "win")),
        P(),
        P(("groups", "win")),
        P(("groups", "chan")),
    )
    out_specs = P(("groups", "win"), "chan", None)
    return jax.shard_map(body, mesh=mesh, in_specs=in_specs, out_specs=out_specs, check_vma=False)
```

profile of v0, /device:TPU:0, one launch (start us, length us, event | category | flops | bytes accessed | tf_op | source)
XLA Modules:
  0.0 139.5 jit_solution(8627850086978740682)
XLA Ops:
  6.5 0.7 fusion.47
  7.3 0.6 reduce-window.6
  7.8 0.2 slice_reduce_fusion
  8.1 0.1 fusion.44
  8.2 1.4 %scatter_custom_fusion = s32[512]{0:T(512)S(1)} fusion(s32[256]{0:T(256)S(1)} %compare_select_fusion.2, s32[256]{0:T(256)S(1)} %get-tuple-element.40, s32[]{:T(128)} %constant.101.clone.1), kind=kCustom, calls=%fused_computation.92 | custom fusion | bytes 2052 | tf_op jit(solution)/shard_map/scatter | solution.py:108
  9.6 0.7 all_to_all.9
  10.3 7.3 %all-to-all-start = ((s32[8,1,64]{2,1,0:T(1,128)}), s32[8,1,64]{2,1,0:T(1,128)S(1)}, u32[]{:S(2)}, u32[]{:S(2)}) async-start(s32[8,1,64]{2,1,0:T(1,128)} %all_to_all.9), calls=%async_computation | async-start | bytes 8192 | tf_op jit(solution)/shard_map/all_to_all | solution.py:120
  17.6 0.7 fusion.50
  18.2 2.9 %fusion.34 = (f32[512,256]{1,0:T(8,128)}, f32[512,256]{1,0:T(8,128)}) fusion(s32[256]{0:T(256)S(1)} %iota_add_fusion), kind=kLoop, calls=%fused_computation.58 | loop fusion | flops 1966080 | bytes 1049600 | tf_op jit(solution)/shard_map/cos | solution.py:56
  21.2 0.1 subtract_select_fusion
  21.3 0.1 convert_reduce_fusion
  21.4 0.7 convert_element_type.55
  22.8 2.7 %scatter_custom_fusion.1 = bf16[512,512]{1,0:T(8,128)(2,1)} fusion(s32[256]{0:T(256)S(1)} %compare_select_fusion.2, bf16[256,512]{1,0:T(8,128)(2,1)} %param.6, bf16[]{:T(256)} %constant.100.clone.1), kind=kCustom, calls=%fused_computation.60 | custom fusion | bytes 524800 | tf_op jit(solution)/shard_map/scatter | solution.py:115
  25.5 6.0 %all-to-all-start.1 = ((bf16[8,64,512]{2,1,0:T(8,128)(2,1)}), bf16[8,64,512]{2,1,0:T(8,128)(2,1)S(1)}, u32[]{:S(2)}, u32[]{:S(2)}) async-start(bf16[8,64,512]{2,1,0:T(8,128)(2,1)} %bitcast.4), calls=%async_computation.1 | async-start | bytes 1048576 | tf_op jit(solution)/shard_map/all_to_all | solution.py:119
  31.6 8.5 %negate_convert_fusion = (bf16[1024,512]{1,0:T(8,128)(2,1)S(1)}, bf16[1024,512]{1,0:T(8,128)(2,1)S(1)}) fusion(), kind=kLoop, calls=%fused_computation.19 | loop fusion | flops 8912896 | bytes 2097152 | tf_op jit(solution)/shard_map/convert.5
  40.1 2.7 %select_reduce_fusion = bf16[512,135]{0,1:T(8,128)(2,1)S(1)} fusion(f32[32]{0:T(128)S(1)} %convert_element_type.55, s32[512,135]{0,1:T(8,128)S(1)} %subtract_select_fusion), kind=kLoop, calls=%fused_computation.5 | loop fusion | flops 6566400 | bytes 414848 | tf_op jit(solution)/shard_map/reduce_sum | solution.py:34
  42.8 0.5 broadcast.282
  43.3 0.7 reduce.5
  44.0 0.1 reshape.182
  44.0 1.4 %all-to-all-done.1 = bf16[8,64,512]{2,1,0:T(8,128)(2,1)S(1)} async-done(((bf16[8,64,512]{2,1,0:T(8,128)(2,1)}), bf16[8,64,512]{2,1,0:T(8,128)(2,1)S(1)}, u32[]{:S(2)}, u32[]{:S(2)}) %all-to-all-start.1) | async-done | bytes 524320 | tf_op jit(solution)/shard_map/all_to_all | solution.py:119
  45.5 2.4 %scatter_custom_fusion.2 = bf16[256,512]{1,0:T(8,128)(2,1)S(1)} fusion(s32[512]{0:T(512)S(1)} %bitcast.62, bf16[512,512]{1,0:T(8,128)(2,1)S(1)} %bitcast.60, bf16[]{:T(256)} %constant.100.clone.1), kind=kCustom, calls=%fused_computation.67 | custom fusion | bytes 262146 | tf_op jit(solution)/shard_map/scatter | solution.py:127
  47.9 0.2 fusion.60
  48.1 0.1 copy.28
  48.2 0.1 copy.37
  48.5 26.9 %while.1 = (s32[]{:T(128)}, f32[16,2048]{1,0:T(8,128)S(1)}, s32[8,2]{0,1:T(2,128)S(1)}, f32[8,16,1024]{2,0,1:T(8,128)}, s32[]{:T(128)}, /*index=5*/s32[]{:T(128)}) while((s32[]{:T(128)}, f32[16,2048]{1,0:T(8,128)S(1)}, s32[8,2]{0,1:T(2,128)S(1)}, f32[8,16,1024]{2,0,1:T(8,128)}, s32[]{:T(128)}, /*index=5*/s32[]{:T(128)}) %tuple.29), condition=%wide.while_cond, body=%wide.while_body.sunk | while | flops 2 | bytes 393321 | solution.py:138
  48.6 0.5 slice.83
  49.1 0.7 dynamic-slice_bitcast_fusion.2
  49.9 2.0 %dynamic-update-slice.3 = f32[8,16,1024]{2,0,1:T(8,128)} dynamic-update-slice(f32[8,16,1024]{2,0,1:T(8,128)} %get-tuple-element.82, f32[1,16,1024]{2,0,1:T(1,128)S(1)} %copy.51, s32[]{:T(128)} %get-tuple-element.79, s32[]{:T(128)} %constant.103.clone.1..sunk, s32[]{:T(128)} %constant.103.clone.1..sunk) | dynamic-update-slice | bytes 131076 | tf_op jit(solution)/shard_map/vmap()/gather
  51.9 0.5 slice.83
  52.4 0.7 dynamic-slice_bitcast_fusion.2
  53.2 2.0 %dynamic-update-slice.3 = f32[8,16,1024]{2,0,1:T(8,128)} dynamic-update-slice(f32[8,16,1024]{2,0,1:T(8,128)} %get-tuple-element.82, f32[1,16,1024]{2,0,1:T(1,128)S(1)} %copy.51, s32[]{:T(128)} %get-tuple-element.79, s32[]{:T(128)} %constant.103.clone.1..sunk, s32[]{:T(128)} %constant.103.clone.1..sunk) | dynamic-update-slice | bytes 131076 | tf_op jit(solution)/shard_map/vmap()/gather
  55.3 0.5 slice.83
  55.8 0.7 dynamic-slice_bitcast_fusion.2
  56.6 2.0 %dynamic-update-slice.3 = f32[8,16,1024]{2,0,1:T(8,128)} dynamic-update-slice(f32[8,16,1024]{2,0,1:T(8,128)} %get-tuple-element.82, f32[1,16,1024]{2,0,1:T(1,128)S(1)} %copy.51, s32[]{:T(128)} %get-tuple-element.79, s32[]{:T(128)} %constant.103.clone.1..sunk, s32[]{:T(128)} %constant.103.clone.1..sunk) | dynamic-update-slice | bytes 131076 | tf_op jit(solution)/shard_map/vmap()/gather
  58.7 0.5 slice.83
  59.2 0.7 dynamic-slice_bitcast_fusion.2
  60.0 2.0 %dynamic-update-slice.3 = f32[8,16,1024]{2,0,1:T(8,128)} dynamic-update-slice(f32[8,16,1024]{2,0,1:T(8,128)} %get-tuple-element.82, f32[1,16,1024]{2,0,1:T(1,128)S(1)} %copy.51, s32[]{:T(128)} %get-tuple-element.79, s32[]{:T(128)} %constant.103.clone.1..sunk, s32[]{:T(128)} %constant.103.clone.1..sunk) | dynamic-update-slice | bytes 131076 | tf_op jit(solution)/shard_map/vmap()/gather
  62.0 0.5 slice.83
  62.5 0.7 dynamic-slice_bitcast_fusion.2
  63.3 2.0 %dynamic-update-slice.3 = f32[8,16,1024]{2,0,1:T(8,128)} dynamic-update-slice(f32[8,16,1024]{2,0,1:T(8,128)} %get-tuple-element.82, f32[1,16,1024]{2,0,1:T(1,128)S(1)} %copy.51, s32[]{:T(128)} %get-tuple-element.79, s32[]{:T(128)} %constant.103.clone.1..sunk, s32[]{:T(128)} %constant.103.clone.1..sunk) | dynamic-update-slice | bytes 131076 | tf_op jit(solution)/shard_map/vmap()/gather
  65.4 0.5 slice.83
  65.9 0.7 dynamic-slice_bitcast_fusion.2
  66.7 2.0 %dynamic-update-slice.3 = f32[8,16,1024]{2,0,1:T(8,128)} dynamic-update-slice(f32[8,16,1024]{2,0,1:T(8,128)} %get-tuple-element.82, f32[1,16,1024]{2,0,1:T(1,128)S(1)} %copy.51, s32[]{:T(128)} %get-tuple-element.79, s32[]{:T(128)} %constant.103.clone.1..sunk, s32[]{:T(128)} %constant.103.clone.1..sunk) | dynamic-update-slice | bytes 131076 | tf_op jit(solution)/shard_map/vmap()/gather
  68.7 0.5 slice.83
  69.3 0.7 dynamic-slice_bitcast_fusion.2
  70.1 2.0 %dynamic-update-slice.3 = f32[8,16,1024]{2,0,1:T(8,128)} dynamic-update-slice(f32[8,16,1024]{2,0,1:T(8,128)} %get-tuple-element.82, f32[1,16,1024]{2,0,1:T(1,128)S(1)} %copy.51, s32[]{:T(128)} %get-tuple-element.79, s32[]{:T(128)} %constant.103.clone.1..sunk, s32[]{:T(128)} %constant.103.clone.1..sunk) | dynamic-update-slice | bytes 131076 | tf_op jit(solution)/shard_map/vmap()/gather
  72.1 0.5 slice.83
  72.6 0.7 dynamic-slice_bitcast_fusion.2
  73.4 2.0 %dynamic-update-slice.3 = f32[8,16,1024]{2,0,1:T(8,128)} dynamic-update-slice(f32[8,16,1024]{2,0,1:T(8,128)} %get-tuple-element.82, f32[1,16,1024]{2,0,1:T(1,128)S(1)} %copy.51, s32[]{:T(128)} %get-tuple-element.79, s32[]{:T(128)} %constant.103.clone.1..sunk, s32[]{:T(128)} %constant.103.clone.1..sunk) | dynamic-update-slice | bytes 131076 | tf_op jit(solution)/shard_map/vmap()/gather
  75.4 1.5 %fusion.3 = f32[128,1024]{1,0:T(8,128)S(1)} fusion(bf16[1024,512]{1,0:T(8,128)(2,1)S(1)} %get-tuple-element.46, bf16[1024,512]{1,0:T(8,128)(2,1)S(1)} %get-tuple-element.47, f32[8,16,1024]{2,0,1:T(8,128)} %get-tuple-element.27, f32[1024]{0:T(1024)S(1)} %multiply_subtract_fusion), kind=kOutput, calls=%fused_computation.13 | convolution fusion | flops 272891904 | bytes 3149824 | tf_op jit(solution)/shard_map/dot_general | solution.py:142
  76.9 0.5 fusion.13
  77.6 30.8 %all_gather.3 = bf16[8,8,1024]{2,1,0:T(8,128)(2,1)S(1)} all-gather(bf16[1,8,1024]{2,1,0:T(8,128)(2,1)S(1)} %constant_dynamic-slice_fusion.1), channel_id=1, replica_groups=mesh['groups'=2,'chan'=8,'win'=2] {'chan'}, dimensions={0}, use_global_device_ids=true | all-gather | bytes 147456 | tf_op jit(solution)/shard_map/all_gather | solution.py:145
  108.4 0.7 copy.41
  109.1 1.7 %copy.40 = bf16[16,8,512]{0,1,2:T(8,128)(2,1)} copy(bf16[16,8,512]{2,1,0:T(8,128)(2,1)S(1)} %get-tuple-element.37) | data formatting | bytes 262144
  110.8 0.7 copy.43
  111.5 0.8 copy.42
  112.4 2.0 %fusion.58 = f32[512,16,8]{1,2,0:T(8,128)S(1)} fusion(bf16[16,8,512]{0,1,2:T(8,128)(2,1)} %copy.40, bf16[8,8,512]{1,0,2:T(8,128)(2,1)S(1)} %copy.41), kind=kOutput, calls=%fused_computation.105 | convolution fusion | flops 1048576 | bytes 458752 | tf_op jit(solution)/shard_map/while/body/eval_jaxpr/bwf,cwf->bcf/dot_general | solution.py:76
  114.4 2.0 %fusion.59 = f32[512,16,8]{1,2,0:T(8,128)} fusion(bf16[16,8,512]{0,1,2:T(8,128)(2,1)S(1)} %copy-done, bf16[8,8,512]{1,0,2:T(8,128)(2,1)S(1)} %copy.43), kind=kOutput, calls=%fused_computation.106 | convolution fusion | flops 1048576 | bytes 458752 | tf_op jit(solution)/shard_map/while/body/eval_jaxpr/bwf,cwf->bcf/dot_general | solution.py:79
  116.4 1.7 %fusion.10 = bf16[8,16,512]{1,0,2:T(8,128)(2,1)} fusion(f32[512,16,8]{1,2,0:T(8,128)S(1)} %fusion.58, bf16[16,8,512]{0,1,2:T(8,128)(2,1)S(1)} %copy.42, bf16[8,8,512]{1,0,2:T(8,128)(2,1)S(1)} %copy.43), kind=kOutput, calls=%fused_computation.24 | convolution fusion | flops 1179648 | bytes 589824 | tf_op jit(solution)/shard_map/while/body/eval_jaxpr/bwf,cwf->bcf/dot_general | solution.py:78
  118.1 1.8 %copy.35 = bf16[8,16,512]{2,1,0:T(8,128)(2,1)S(1)} copy(bf16[8,16,512]{1,0,2:T(8,128)(2,1)} %fusion.10) | data formatting | bytes 262144 | tf_op jit(solution)/shard_map/while/body/eval_jaxpr/add | solution.py:76
  120.0 2.3 %fusion.11 = bf16[8,16,512]{1,0,2:T(8,128)(2,1)S(1)} fusion(f32[512,16,8]{1,2,0:T(8,128)} %fusion.59, bf16[16,8,512]{0,1,2:T(8,128)(2,1)S(1)} %copy.42, bf16[8,8,512]{1,0,2:T(8,128)(2,1)S(1)} %copy.41), kind=kOutput, calls=%fused_computation.25 | convolution fusion | flops 1179648 | bytes 589824 | tf_op jit(solution)/shard_map/while/body/eval_jaxpr/bwf,cwf->bcf/dot_general | solution.py:81
  122.2 0.7 copy.36
  123.0 2.1 %fusion.19 = f32[8,16,256]{2,1,0:T(8,128)} fusion(f32[512,256]{1,0:T(8,128)} %get-tuple-element.43, f32[512,256]{1,0:T(8,128)} %get-tuple-element.42, bf16[8,16,512]{2,1,0:T(8,128)(2,1)S(1)} %copy.36, bf16[8,16,512]{2,1,0:T(8,128)(2,1)S(1)} %copy.35), kind=kOutput, calls=%fused_computation.40 | convolution fusion | flops 68419584 | bytes 1441792 | tf_op jit(solution)/shard_map/while/body/eval_jaxpr/dot_general | solution.py:150
  125.1 7.6 %reduce-scatter.2.cloned.1.call-done = f32[4,16,256]{2,1,0:T(8,128)} async-done(((f32[8,16,256]{2,1,0:T(8,128)}), f32[4,16,256]{2,1,0:T(8,128)}) %reduce-scatter.2.cloned.1.call-update) | async-done | bytes 65552 | tf_op jit(solution)/shard_map/reduce_scatter | solution.py:154
  (40 shorter events, 1.5 us)
Async XLA Ops:
  10.3 15.2 %all-to-all-start = ((s32[8,1,64]{2,1,0:T(1,128)}), s32[8,1,64]{2,1,0:T(1,128)S(1)}, u32[]{:S(2)}, u32[]{:S(2)}) async-start(s32[8,1,64]{2,1,0:T(1,128)} %all_to_all.9), calls=%async_computation | async-start | bytes 8192 | tf_op jit(solution)/shard_map/all_to_all | solution.py:120
  25.5 20.0 %all-to-all-start.1 = ((bf16[8,64,512]{2,1,0:T(8,128)(2,1)}), bf16[8,64,512]{2,1,0:T(8,128)(2,1)S(1)}, u32[]{:S(2)}, u32[]{:S(2)}) async-start(bf16[8,64,512]{2,1,0:T(8,128)(2,1)} %bitcast.4), calls=%async_computation.1 | async-start | bytes 1048576 | tf_op jit(solution)/shard_map/all_to_all | solution.py:119
  31.5 101.2 %reduce-scatter.2.cloned.1.call-start = ((), (), s32[]{:S(2)}) async-start(), calls=%async_computation.3 | async-start | bytes 196608 | tf_op jit(solution)/shard_map/reduce_scatter | solution.py:154
  112.4 2.0 %copy-start = (bf16[16,8,512]{0,1,2:T(8,128)(2,1)S(1)}, bf16[16,8,512]{0,1,2:T(8,128)(2,1)}, u32[]{:S(2)}) copy-start(bf16[16,8,512]{0,1,2:T(8,128)(2,1)} %copy.40) | copy-start | bytes 393220
Sparse Core Ops, SparseCore 0:
  125.2 7.4 reduce-scatter.1
where the time goes:
time: 140 us; the launch traced here: 139 us
  local copies, waits for them, and re-layouts  41.7 us (30%)
  blocking collectives  30.8 us (22%)
  other arithmetic  18 us (13%)
  between operations  14.3 us (10%)
  starting transfers between devices  13.3 us (10%)
  matrix products  12.4 us (9%)
  waiting for transfers between devices  9 us (6%)
    all_gather x1, blocking collectives, body(): gathered = lax.all_gather(source, 'chan', axis=0, tiled=True)  30.8 us
    gather x40, local copies, waits for them, and re-layouts  26.8 us
    another operation x3, other arithmetic  9.17 us
    reduce_scatter x1, waiting for transfers between devices, body(): lax.psum_scatter(over_blocks(span_block, gathered, CH_DEV), 'win', scatte...  7.58 us
    all_to_all x1, starting transfers between devices, body(): lax.all_to_all(slot_table, 'chan', split_axis=0, concat_axis=0, tiled=True)  7.25 us
    all_to_all x1, starting transfers between devices, body(): lax.all_to_all(row_send, 'chan', split_axis=0, concat_axis=0, tiled=True)  5.99 us
    unnamed x7, local copies, waits for them, and re-layouts  4.01 us
    cos x1, other arithmetic, make_lags(): jnp.cos(phase)  2.94 us
  transfers between devices with their start and end apart: 3, of which 2 were waited for; matrix products, arithmetic and copies ran while one was open for 14% of the time, Pallas kernels for 0%

commit v1 on v0

--- a/solution.py
+++ b/solution.py
@@ -142,7 +142,12 @@
     spectra = jnp.dot(segments.reshape(-1, WL), make_fourier(), preferred_element_type=jnp.float32)
     whitened = whiten(spectra).reshape(CH_DEV, window_count, WL)
     source = lax.dynamic_slice_in_dim(whitened, source_slot[0], 1, 0)
-    gathered = lax.all_gather(source, "chan", axis=0, tiled=True)
+    ring = [source]
+    for hop in range(7):
+        ring.append(lax.ppermute(ring[-1], "chan", [(dev, (dev + 1) % 8) for dev in range(8)]))
+    gathered = jnp.roll(
+        jnp.concatenate(ring[::-1], axis=0), (lax.axis_index("chan") + 1) * ring[0].shape[0], axis=0
+    )
     lag_table = make_lags()
 
     def span_block(source_block):

time: 140 us -> 147 us (1.050)
  waiting for transfers between devices: 9 us -> 46.2 us
  blocking collectives: 30.8 us -> 0 us
    ppermute x0 -> x7, waiting for transfers between devices: none -> 38.1 us  [body(): lax.ppermute(ring[-1], 'chan', [(dev, (dev + 1) % 8) for dev in range(8)])]
    all_gather x1 -> x0, blocking collectives: 30.8 us -> none  [body(): gathered = lax.all_gather(source, 'chan', axis=0, tiled=True)]
    reduce_scatter x1, waiting for transfers between devices: 7.58 us -> 5.25 us  [body(): lax.psum_scatter(over_blocks(span_block, gathered, CH_DEV), 'win', scatte...]
    ppermute x0 -> x7, starting transfers between devices: none -> 1.49 us  [body(): lax.ppermute(ring[-1], 'chan', [(dev, (dev + 1) % 8) for dev in range(8)])]
    unnamed x7 -> x22, local copies, waits for them, and re-layouts: 4.01 us -> 4.07 us
  transfers between devices with their start and end apart: 3 -> 10, of which waited for: 2 -> 10; matrix products, arithmetic and copies ran while one was open for 14% -> 15% of each run, Pallas kernels for 0% -> 0%
where the time goes in v1:
time: 147 us; the launch traced here: 146 us
  waiting for transfers between devices  46.2 us (31%)
  local copies, waits for them, and re-layouts  41.8 us (28%)
  other arithmetic  18 us (12%)
  between operations  14.4 us (10%)
  starting transfers between devices  13.4 us (9%)
  matrix products  12.4 us (8%)
    ppermute x7, waiting for transfers between devices, body(): lax.ppermute(ring[-1], 'chan', [(dev, (dev + 1) % 8) for dev in range(8)])  38.1 us
    gather x40, local copies, waits for them, and re-layouts  26.8 us
    another operation x3, other arithmetic  9.17 us
    all_to_all x1, starting transfers between devices, body(): lax.all_to_all(slot_table, 'chan', split_axis=0, concat_axis=0, tiled=True)  7.25 us
    reduce_scatter x1, waiting for transfers between devices, body(): lax.psum_scatter(over_blocks(span_block, gathered, CH_DEV), 'win', scatte...  5.25 us
    all_to_all x1, starting transfers between devices, body(): lax.all_to_all(row_send, 'chan', split_axis=0, concat_axis=0, tiled=True)  4.61 us
    unnamed x22, local copies, waits for them, and re-layouts  4.07 us
    cos x1, other arithmetic, make_lags(): jnp.cos(phase)  2.94 us
  transfers between devices with their start and end apart: 10, of which 10 were waited for; matrix products, arithmetic and copies ran while one was open for 15% of the time, Pallas kernels for 0%

profile of v1, /device:TPU:0, one launch (start us, length us, event | category | flops | bytes accessed | tf_op | source)
XLA Modules:
  0.0 146.2 jit_solution(14580259381969612008)
XLA Ops:
  6.5 0.7 fusion.47
  7.3 0.6 reduce-window.6
  8.2 1.4 scatter_custom_fusion
  9.6 0.7 all_to_all.9
  10.3 7.3 %all-to-all-start = ((s32[8,1,64]{2,1,0:T(1,128)}), s32[8,1,64]{2,1,0:T(1,128)S(1)}, u32[]{:S(2)}, u32[]{:S(2)}) async-start(s32[8,1,64]{2,1,0:T(1,128)} %all_to_all.9), calls=%async_computation | async-start | bytes 8192 | tf_op jit(solution)/shard_map/all_to_all | solution.py:120
  17.6 0.7 fusion.50
  18.5 0.7 convert_element_type.55
  19.8 2.7 %scatter_custom_fusion.1 = bf16[512,512]{1,0:T(8,128)(2,1)} fusion(s32[256]{0:T(256)S(1)} %compare_select_fusion.2, bf16[256,512]{1,0:T(8,128)(2,1)} %param.6, bf16[]{:T(256)} %constant.123.clone.1), kind=kCustom, calls=%fused_computation.60 | custom fusion | bytes 524800 | tf_op jit(solution)/shard_map/scatter | solution.py:115
  22.5 1.4 all-to-all-done
  23.9 4.6 %all-to-all-start.1 = ((bf16[8,64,512]{2,1,0:T(8,128)(2,1)}), bf16[8,64,512]{2,1,0:T(8,128)(2,1)S(1)}, u32[]{:S(2)}, u32[]{:S(2)}) async-start(bf16[8,64,512]{2,1,0:T(8,128)(2,1)} %bitcast.4), calls=%async_computation.1 | async-start | bytes 1048576 | tf_op jit(solution)/shard_map/all_to_all | solution.py:119
  28.6 8.5 %negate_convert_fusion = (bf16[1024,512]{1,0:T(8,128)(2,1)S(1)}, bf16[1024,512]{1,0:T(8,128)(2,1)S(1)}) fusion(), kind=kLoop, calls=%fused_computation.19 | loop fusion | flops 8912896 | bytes 2097152 | tf_op jit(solution)/shard_map/convert.5
  37.2 2.7 %select_reduce_fusion = bf16[512,135]{0,1:T(8,128)(2,1)S(1)} fusion(f32[32]{0:T(128)S(1)} %convert_element_type.55, s32[512,135]{0,1:T(8,128)S(1)} %subtract_select_fusion), kind=kLoop, calls=%fused_computation.5 | loop fusion | flops 6566400 | bytes 414848 | tf_op jit(solution)/shard_map/reduce_sum | solution.py:34
  39.8 0.5 broadcast.283
  40.3 0.7 reduce.5
  41.1 1.4 all-to-all-done.1
  42.5 2.4 %scatter_custom_fusion.2 = bf16[256,512]{1,0:T(8,128)(2,1)S(1)} fusion(s32[512]{0:T(512)S(1)} %bitcast.62, bf16[512,512]{1,0:T(8,128)(2,1)S(1)} %bitcast.60, bf16[]{:T(256)} %constant.123.clone.1), kind=kCustom, calls=%fused_computation.67 | custom fusion | bytes 262146 | tf_op jit(solution)/shard_map/scatter | solution.py:127
  45.5 26.9 %while.1 = (s32[]{:T(128)}, f32[16,2048]{1,0:T(8,128)S(1)}, s32[8,2]{0,1:T(2,128)S(1)}, f32[8,16,1024]{2,0,1:T(8,128)}, s32[]{:T(128)}, /*index=5*/s32[]{:T(128)}) while((s32[]{:T(128)}, f32[16,2048]{1,0:T(8,128)S(1)}, s32[8,2]{0,1:T(2,128)S(1)}, f32[8,16,1024]{2,0,1:T(8,128)}, s32[]{:T(128)}, /*index=5*/s32[]{:T(128)}) %tuple.29), condition=%wide.while_cond, body=%wide.while_body.sunk | while | flops 2 | bytes 393321 | solution.py:138
  45.6 0.5 slice.79
  46.1 0.7 dynamic-slice_bitcast_fusion.2
  46.9 2.0 %dynamic-update-slice.35 = f32[8,16,1024]{2,0,1:T(8,128)} dynamic-update-slice(f32[8,16,1024]{2,0,1:T(8,128)} %get-tuple-element.82, f32[1,16,1024]{2,0,1:T(1,128)S(1)} %copy.41, s32[]{:T(128)} %get-tuple-element.79, s32[]{:T(128)} %constant.126.clone.1..sunk, s32[]{:T(128)} %constant.126.clone.1..sunk) | dynamic-update-slice | bytes 131076 | tf_op jit(solution)/shard_map/vmap()/gather
  49.0 0.5 slice.79
  49.5 0.7 dynamic-slice_bitcast_fusion.2
  50.3 2.0 %dynamic-update-slice.35 = f32[8,16,1024]{2,0,1:T(8,128)} dynamic-update-slice(f32[8,16,1024]{2,0,1:T(8,128)} %get-tuple-element.82, f32[1,16,1024]{2,0,1:T(1,128)S(1)} %copy.41, s32[]{:T(128)} %get-tuple-element.79, s32[]{:T(128)} %constant.126.clone.1..sunk, s32[]{:T(128)} %constant.126.clone.1..sunk) | dynamic-update-slice | bytes 131076 | tf_op jit(solution)/shard_map/vmap()/gather
  52.3 0.5 slice.79
  52.9 0.7 dynamic-slice_bitcast_fusion.2
  53.7 2.0 %dynamic-update-slice.35 = f32[8,16,1024]{2,0,1:T(8,128)} dynamic-update-slice(f32[8,16,1024]{2,0,1:T(8,128)} %get-tuple-element.82, f32[1,16,1024]{2,0,1:T(1,128)S(1)} %copy.41, s32[]{:T(128)} %get-tuple-element.79, s32[]{:T(128)} %constant.126.clone.1..sunk, s32[]{:T(128)} %constant.126.clone.1..sunk) | dynamic-update-slice | bytes 131076 | tf_op jit(solution)/shard_map/vmap()/gather
  55.7 0.5 slice.79
  56.2 0.7 dynamic-slice_bitcast_fusion.2
  57.0 2.0 %dynamic-update-slice.35 = f32[8,16,1024]{2,0,1:T(8,128)} dynamic-update-slice(f32[8,16,1024]{2,0,1:T(8,128)} %get-tuple-element.82, f32[1,16,1024]{2,0,1:T(1,128)S(1)} %copy.41, s32[]{:T(128)} %get-tuple-element.79, s32[]{:T(128)} %constant.126.clone.1..sunk, s32[]{:T(128)} %constant.126.clone.1..sunk) | dynamic-update-slice | bytes 131076 | tf_op jit(solution)/shard_map/vmap()/gather
  59.1 0.5 slice.79
  59.6 0.7 dynamic-slice_bitcast_fusion.2
  60.4 2.0 %dynamic-update-slice.35 = f32[8,16,1024]{2,0,1:T(8,128)} dynamic-update-slice(f32[8,16,1024]{2,0,1:T(8,128)} %get-tuple-element.82, f32[1,16,1024]{2,0,1:T(1,128)S(1)} %copy.41, s32[]{:T(128)} %get-tuple-element.79, s32[]{:T(128)} %constant.126.clone.1..sunk, s32[]{:T(128)} %constant.126.clone.1..sunk) | dynamic-update-slice | bytes 131076 | tf_op jit(solution)/shard_map/vmap()/gather
  62.4 0.5 slice.79
  63.0 0.7 dynamic-slice_bitcast_fusion.2
  63.8 2.0 %dynamic-update-slice.35 = f32[8,16,1024]{2,0,1:T(8,128)} dynamic-update-slice(f32[8,16,1024]{2,0,1:T(8,128)} %get-tuple-element.82, f32[1,16,1024]{2,0,1:T(1,128)S(1)} %copy.41, s32[]{:T(128)} %get-tuple-element.79, s32[]{:T(128)} %constant.126.clone.1..sunk, s32[]{:T(128)} %constant.126.clone.1..sunk) | dynamic-update-slice | bytes 131076 | tf_op jit(solution)/shard_map/vmap()/gather
  65.8 0.5 slice.79
  66.3 0.7 dynamic-slice_bitcast_fusion.2
  67.1 2.0 %dynamic-update-slice.35 = f32[8,16,1024]{2,0,1:T(8,128)} dynamic-update-slice(f32[8,16,1024]{2,0,1:T(8,128)} %get-tuple-element.82, f32[1,16,1024]{2,0,1:T(1,128)S(1)} %copy.41, s32[]{:T(128)} %get-tuple-element.79, s32[]{:T(128)} %constant.126.clone.1..sunk, s32[]{:T(128)} %constant.126.clone.1..sunk) | dynamic-update-slice | bytes 131076 | tf_op jit(solution)/shard_map/vmap()/gather
  69.2 0.5 slice.79
  69.7 0.7 dynamic-slice_bitcast_fusion.2
  70.5 2.0 %dynamic-update-slice.35 = f32[8,16,1024]{2,0,1:T(8,128)} dynamic-update-slice(f32[8,16,1024]{2,0,1:T(8,128)} %get-tuple-element.82, f32[1,16,1024]{2,0,1:T(1,128)S(1)} %copy.41, s32[]{:T(128)} %get-tuple-element.79, s32[]{:T(128)} %constant.126.clone.1..sunk, s32[]{:T(128)} %constant.126.clone.1..sunk) | dynamic-update-slice | bytes 131076 | tf_op jit(solution)/shard_map/vmap()/gather
  72.5 1.5 %fusion.3 = f32[128,1024]{1,0:T(8,128)S(1)} fusion(bf16[1024,512]{1,0:T(8,128)(2,1)S(1)} %get-tuple-element.46, bf16[1024,512]{1,0:T(8,128)(2,1)S(1)} %get-tuple-element.47, f32[8,16,1024]{2,0,1:T(8,128)} %get-tuple-element.27, f32[1024]{0:T(1024)S(1)} %multiply_subtract_fusion), kind=kOutput, calls=%fused_computation.13 | convolution fusion | flops 272891904 | bytes 3149824 | tf_op jit(solution)/shard_map/dot_general | solution.py:142
  73.9 0.5 fusion.13
  74.6 1.5 %collective-permute-start = (bf16[1,8,1024]{2,1,0:T(8,128)(2,1)S(1)}, bf16[1,8,1024]{2,1,0:T(8,128)(2,1)S(1)}, u32[]{:S(2)}, u32[]{:S(2)}) collective-permute-start(bf16[1,8,1024]{2,1,0:T(8,128)(2,1)S(1)} %constant_dynamic-slice_fusion.3), channel_id=1, source_target_pairs={{0,2},{2,4},{4,6},{6,8},{8,10},{10,12},{12,14},{14,0},{1,3},{3,5},... | collective-permute-start | bytes 49160 | tf_op jit(solution)/shard_map/ppermute | solution.py:147
  76.1 5.0 %collective-permute-done = bf16[1,8,1024]{2,1,0:T(8,128)(2,1)S(1)} collective-permute-done((bf16[1,8,1024]{2,1,0:T(8,128)(2,1)S(1)}, bf16[1,8,1024]{2,1,0:T(8,128)(2,1)S(1)}, u32[]{:S(2)}, u32[]{:S(2)}) %collective-permute-start) | collective-permute-done | bytes 16416 | tf_op jit(solution)/shard_map/ppermute | solution.py:147
  81.1 6.4 %collective-permute-done.1 = bf16[1,8,1024]{2,1,0:T(8,128)(2,1)S(1)} collective-permute-done((bf16[1,8,1024]{2,1,0:T(8,128)(2,1)S(1)}, bf16[1,8,1024]{2,1,0:T(8,128)(2,1)S(1)}, u32[]{:S(2)}, u32[]{:S(2)}) %collective-permute-start.1) | collective-permute-done | bytes 16416 | tf_op jit(solution)/shard_map/ppermute | solution.py:147
  87.5 6.4 %collective-permute-done.2 = bf16[1,8,1024]{2,1,0:T(8,128)(2,1)S(1)} collective-permute-done((bf16[1,8,1024]{2,1,0:T(8,128)(2,1)S(1)}, bf16[1,8,1024]{2,1,0:T(8,128)(2,1)S(1)}, u32[]{:S(2)}, u32[]{:S(2)}) %collective-permute-start.2) | collective-permute-done | bytes 16416 | tf_op jit(solution)/shard_map/ppermute | solution.py:147
  93.9 6.4 %collective-permute-done.3 = bf16[1,8,1024]{2,1,0:T(8,128)(2,1)S(1)} collective-permute-done((bf16[1,8,1024]{2,1,0:T(8,128)(2,1)S(1)}, bf16[1,8,1024]{2,1,0:T(8,128)(2,1)S(1)}, u32[]{:S(2)}, u32[]{:S(2)}) %collective-permute-start.3) | collective-permute-done | bytes 16416 | tf_op jit(solution)/shard_map/ppermute | solution.py:147
  100.4 6.4 %collective-permute-done.4 = bf16[1,8,1024]{2,1,0:T(8,128)(2,1)S(1)} collective-permute-done((bf16[1,8,1024]{2,1,0:T(8,128)(2,1)S(1)}, bf16[1,8,1024]{2,1,0:T(8,128)(2,1)S(1)}, u32[]{:S(2)}, u32[]{:S(2)}) %collective-permute-start.4) | collective-permute-done | bytes 16416 | tf_op jit(solution)/shard_map/ppermute | solution.py:147
  106.8 2.9 %fusion.34 = (f32[512,256]{1,0:T(8,128)}, f32[512,256]{1,0:T(8,128)}) fusion(s32[256]{0:T(256)S(1)} %iota_add_fusion), kind=kLoop, calls=%fused_computation.58 | loop fusion | flops 1966080 | bytes 1049600 | tf_op jit(solution)/shard_map/cos | solution.py:56
  109.8 3.5 %collective-permute-done.5 = bf16[1,8,1024]{2,1,0:T(8,128)(2,1)S(1)} collective-permute-done((bf16[1,8,1024]{2,1,0:T(8,128)(2,1)S(1)}, bf16[1,8,1024]{2,1,0:T(8,128)(2,1)S(1)}, u32[]{:S(2)}, u32[]{:S(2)}) %collective-permute-start.5) | collective-permute-done | bytes 16416 | tf_op jit(solution)/shard_map/ppermute | solution.py:147
  113.3 1.7 %copy.32 = bf16[16,8,512]{0,1,2:T(8,128)(2,1)} copy(bf16[16,8,512]{2,1,0:T(8,128)(2,1)S(1)} %get-tuple-element.39) | data formatting | bytes 262144
  115.0 0.8 copy.29
  115.8 3.9 %collective-permute-done.6 = bf16[1,8,1024]{2,1,0:T(8,128)(2,1)S(1)} collective-permute-done((bf16[1,8,1024]{2,1,0:T(8,128)(2,1)S(1)}, bf16[1,8,1024]{2,1,0:T(8,128)(2,1)S(1)}, u32[]{:S(2)}, u32[]{:S(2)}) %collective-permute-start.6) | collective-permute-done | bytes 16416 | tf_op jit(solution)/shard_map/ppermute | solution.py:147
  119.9 0.7 copy.33
  120.6 0.7 copy.31
  121.4 2.0 %fusion.57 = f32[512,16,8]{1,2,0:T(8,128)S(1)} fusion(bf16[16,8,512]{0,1,2:T(8,128)(2,1)} %copy.32, bf16[8,8,512]{1,0,2:T(8,128)(2,1)S(1)} %copy.33), kind=kOutput, calls=%fused_computation.122 | convolution fusion | flops 1048576 | bytes 458752 | tf_op jit(solution)/shard_map/while/body/eval_jaxpr/bwf,cwf->bcf/dot_general | solution.py:78
  123.4 2.0 %fusion.58 = f32[512,16,8]{1,2,0:T(8,128)} fusion(bf16[16,8,512]{0,1,2:T(8,128)(2,1)S(1)} %copy-done, bf16[8,8,512]{1,0,2:T(8,128)(2,1)S(1)} %copy.31), kind=kOutput, calls=%fused_computation.123 | convolution fusion | flops 1048576 | bytes 458752 | tf_op jit(solution)/shard_map/while/body/eval_jaxpr/bwf,cwf->bcf/dot_general | solution.py:81
  125.4 1.7 %fusion.10 = bf16[8,16,512]{1,0,2:T(8,128)(2,1)} fusion(f32[512,16,8]{1,2,0:T(8,128)S(1)} %fusion.57, bf16[16,8,512]{0,1,2:T(8,128)(2,1)S(1)} %copy.29, bf16[8,8,512]{1,0,2:T(8,128)(2,1)S(1)} %copy.31), kind=kOutput, calls=%fused_computation.24 | convolution fusion | flops 1179648 | bytes 589824 | tf_op jit(solution)/shard_map/while/body/eval_jaxpr/bwf,cwf->bcf/dot_general | solution.py:76
  127.1 1.8 %copy.24 = bf16[8,16,512]{2,1,0:T(8,128)(2,1)S(1)} copy(bf16[8,16,512]{1,0,2:T(8,128)(2,1)} %fusion.10) | data formatting | bytes 262144 | tf_op jit(solution)/shard_map/while/body/eval_jaxpr/add | solution.py:76
  129.0 2.3 %fusion.11 = bf16[8,16,512]{1,0,2:T(8,128)(2,1)S(1)} fusion(f32[512,16,8]{1,2,0:T(8,128)} %fusion.58, bf16[16,8,512]{0,1,2:T(8,128)(2,1)S(1)} %copy.29, bf16[8,8,512]{1,0,2:T(8,128)(2,1)S(1)} %copy.33), kind=kOutput, calls=%fused_computation.25 | convolution fusion | flops 1179648 | bytes 589824 | tf_op jit(solution)/shard_map/while/body/eval_jaxpr/bwf,cwf->bcf/dot_general | solution.py:79
  131.2 0.7 copy.25
  131.9 2.1 %fusion.19 = f32[8,16,256]{2,1,0:T(8,128)} fusion(f32[512,256]{1,0:T(8,128)} %get-tuple-element.43, f32[512,256]{1,0:T(8,128)} %get-tuple-element.42, bf16[8,16,512]{2,1,0:T(8,128)(2,1)S(1)} %copy.25, bf16[8,16,512]{2,1,0:T(8,128)(2,1)S(1)} %copy.24), kind=kOutput, calls=%fused_computation.40 | convolution fusion | flops 68419584 | bytes 1441792 | tf_op jit(solution)/shard_map/while/body/eval_jaxpr/dot_general | solution.py:155
  134.1 5.3 %reduce-scatter.2.cloned.1.call-done = f32[4,16,256]{2,1,0:T(8,128)} async-done(((f32[8,16,256]{2,1,0:T(8,128)}), f32[4,16,256]{2,1,0:T(8,128)}) %reduce-scatter.2.cloned.1.call-update) | async-done | bytes 65552 | tf_op jit(solution)/shard_map/reduce_scatter | solution.py:159
  (69 shorter events, 2.7 us)
Async XLA Ops:
  10.3 13.6 %all-to-all-start = ((s32[8,1,64]{2,1,0:T(1,128)}), s32[8,1,64]{2,1,0:T(1,128)S(1)}, u32[]{:S(2)}, u32[]{:S(2)}) async-start(s32[8,1,64]{2,1,0:T(1,128)} %all_to_all.9), calls=%async_computation | async-start | bytes 8192 | tf_op jit(solution)/shard_map/all_to_all | solution.py:120
  23.9 18.6 %all-to-all-start.1 = ((bf16[8,64,512]{2,1,0:T(8,128)(2,1)}), bf16[8,64,512]{2,1,0:T(8,128)(2,1)S(1)}, u32[]{:S(2)}, u32[]{:S(2)}) async-start(bf16[8,64,512]{2,1,0:T(8,128)(2,1)} %bitcast.4), calls=%async_computation.1 | async-start | bytes 1048576 | tf_op jit(solution)/shard_map/all_to_all | solution.py:119
  28.5 110.8 %reduce-scatter.2.cloned.1.call-start = ((), (), s32[]{:S(2)}) async-start(), calls=%async_computation.3 | async-start | bytes 196608 | tf_op jit(solution)/shard_map/reduce_scatter | solution.py:159
  74.6 6.5 %collective-permute-start = (bf16[1,8,1024]{2,1,0:T(8,128)(2,1)S(1)}, bf16[1,8,1024]{2,1,0:T(8,128)(2,1)S(1)}, u32[]{:S(2)}, u32[]{:S(2)}) collective-permute-start(bf16[1,8,1024]{2,1,0:T(8,128)(2,1)S(1)} %constant_dynamic-slice_fusion.3), channel_id=1, source_target_pairs={{0,2},{2,4},{4,6},{6,8},{8,10},{10,12},{12,14},{14,0},{1,3},{3,5},... | collective-permute-start | bytes 49160 | tf_op jit(solution)/shard_map/ppermute | solution.py:147
  81.1 6.4 %collective-permute-start.1 = (bf16[1,8,1024]{2,1,0:T(8,128)(2,1)S(1)}, bf16[1,8,1024]{2,1,0:T(8,128)(2,1)S(1)}, u32[]{:S(2)}, u32[]{:S(2)}) collective-permute-start(bf16[1,8,1024]{2,1,0:T(8,128)(2,1)S(1)} %collective-permute-done), channel_id=1, source_target_pairs={{0,2},{2,4},{4,6},{6,8},{8,10},{10,12},{12,14},{14,0},{1,3},{3,5},... | collective-permute-start | bytes 49160 | tf_op jit(solution)/shard_map/ppermute | solution.py:147
  87.5 6.4 %collective-permute-start.2 = (bf16[1,8,1024]{2,1,0:T(8,128)(2,1)S(1)}, bf16[1,8,1024]{2,1,0:T(8,128)(2,1)S(1)}, u32[]{:S(2)}, u32[]{:S(2)}) collective-permute-start(bf16[1,8,1024]{2,1,0:T(8,128)(2,1)S(1)} %collective-permute-done.1), channel_id=1, source_target_pairs={{0,2},{2,4},{4,6},{6,8},{8,10},{10,12},{12,14},{14,0},{1,3},{3,5},... | collective-permute-start | bytes 49160 | tf_op jit(solution)/shard_map/ppermute | solution.py:147
  93.9 6.4 %collective-permute-start.3 = (bf16[1,8,1024]{2,1,0:T(8,128)(2,1)S(1)}, bf16[1,8,1024]{2,1,0:T(8,128)(2,1)S(1)}, u32[]{:S(2)}, u32[]{:S(2)}) collective-permute-start(bf16[1,8,1024]{2,1,0:T(8,128)(2,1)S(1)} %collective-permute-done.2), channel_id=1, source_target_pairs={{0,2},{2,4},{4,6},{6,8},{8,10},{10,12},{12,14},{14,0},{1,3},{3,5},... | collective-permute-start | bytes 49160 | tf_op jit(solution)/shard_map/ppermute | solution.py:147
  100.4 6.4 %collective-permute-start.4 = (bf16[1,8,1024]{2,1,0:T(8,128)(2,1)S(1)}, bf16[1,8,1024]{2,1,0:T(8,128)(2,1)S(1)}, u32[]{:S(2)}, u32[]{:S(2)}) collective-permute-start(bf16[1,8,1024]{2,1,0:T(8,128)(2,1)S(1)} %collective-permute-done.3), channel_id=1, source_target_pairs={{0,2},{2,4},{4,6},{6,8},{8,10},{10,12},{12,14},{14,0},{1,3},{3,5},... | collective-permute-start | bytes 49160 | tf_op jit(solution)/shard_map/ppermute | solution.py:147
  106.8 6.4 %collective-permute-start.5 = (bf16[1,8,1024]{2,1,0:T(8,128)(2,1)S(1)}, bf16[1,8,1024]{2,1,0:T(8,128)(2,1)S(1)}, u32[]{:S(2)}, u32[]{:S(2)}) collective-permute-start(bf16[1,8,1024]{2,1,0:T(8,128)(2,1)S(1)} %collective-permute-done.4), channel_id=1, source_target_pairs={{0,2},{2,4},{4,6},{6,8},{8,10},{10,12},{12,14},{14,0},{1,3},{3,5},... | collective-permute-start | bytes 49160 | tf_op jit(solution)/shard_map/ppermute | solution.py:147
  113.3 6.4 %collective-permute-start.6 = (bf16[1,8,1024]{2,1,0:T(8,128)(2,1)S(1)}, bf16[1,8,1024]{2,1,0:T(8,128)(2,1)S(1)}, u32[]{:S(2)}, u32[]{:S(2)}) collective-permute-start(bf16[1,8,1024]{2,1,0:T(8,128)(2,1)S(1)} %collective-permute-done.5), channel_id=1, source_target_pairs={{0,2},{2,4},{4,6},{6,8},{8,10},{10,12},{12,14},{14,0},{1,3},{3,5},... | collective-permute-start | bytes 49160 | tf_op jit(solution)/shard_map/ppermute | solution.py:147
  121.3 2.0 %copy-start = (bf16[16,8,512]{0,1,2:T(8,128)(2,1)S(1)}, bf16[16,8,512]{0,1,2:T(8,128)(2,1)}, u32[]{:S(2)}) copy-start(bf16[16,8,512]{0,1,2:T(8,128)(2,1)} %copy.32) | copy-start | bytes 393220
Sparse Core Ops, SparseCore 0:
  134.2 5.0 reduce-scatter.1
